TPU v7x, 32 devices: a whole 2x2x4 slice. The times are simulated.
32 devices in a mesh: half: 2 (over core), vocab: 8 (over z, x), tok: 2 (over y).
Axes of the slice: x: 2, y: 2, z: 4, core: 2. Of those that a mesh axis runs over, the one named last changes fastest.
Arguments:
- teacher_hidden: bfloat16 [2048, 8192], P('vocab', ('half', 'tok')), may hold values from -400 to 400
- student_hidden: bfloat16 [2048, 4096], P('vocab', ('half', 'tok')), may hold values from -400 to 400
- teacher_gain: float32 [8192], P(('half', 'tok')), may hold values from 0.5 to 1.5
- student_gain: float32 [4096], P(('half', 'tok')), may hold values from 0.5 to 1.5
- teacher_head: bfloat16 [8192, 16384], P(('half', 'tok'), 'vocab'), may hold values from -1 to 1
- student_head: bfloat16 [4096, 16384], P(('half', 'tok'), 'vocab'), may hold values from -2 to 2
- labels: int32 [2048], P(('half', 'tok')), may hold values from 0 to 16383
Outputs:
- token_loss: float32 [2048], P(('half', 'tok'))
- logit_grad: bfloat16 [2048, 16384], P(('half', 'tok'), 'vocab')
All inputs are finite; a program needn't handle non-finite values.
Results may differ from a plain program's by a relative error of at most 0.0068.
Values may be sent and summed in bfloat16 or wider, within the bound.
No kernel may reach another device: no remote copies, remote signals or barrier semaphores. Data moves between devices by JAX's collectives and lax.ppermute only.
A program may use at most 192 MiB of HBM per device.

v0:
```python
import jax
import jax.numpy as jnp
from jax import lax
from jax.experimental import pallas as pl
from jax.experimental.pallas import tpu as pltpu
from jax.sharding import PartitionSpec as P


epsilon = 1e-05
label_weight = 0.5
largest_scaled = 400.0 * 1.5
largest_teacher = 1.0
largest_student = 2.0


def wire_scale(depth, largest):
    scale = 1.0
    while depth * largest_scaled * largest * scale > 60000.0:
        scale *= 0.5
    return scale


def product(core, pieces, others, heads, scales, start, total, buffer):
    count = len(pieces)
    rows, depth = pieces[0].shape
    depth_t, depth_s = heads[0].shape[0], heads[1].shape[0]
    columns = heads[2].shape[1]
    tile = min(512 if count == 2 else 256, columns)
    steps = columns // tile
    whole = pl.BlockSpec(memory_space=pltpu.VMEM)

    def body(core, *refs):
        mine, beside = refs[:count], refs[count : 2 * count]
        wt, ws, wt_beside, ws_beside = refs[2 * count : 2 * count + 4]
        out, own, other = refs[-3:]

        @pl.when(pl.program_id(0) == 0)
        def _():
            for k in range(count):
                own[k * rows : (k + 1) * rows] = mine[k][...]
                other[k * rows : (k + 1) * rows] = beside[k][...]

        teacher = jnp.dot(own[:, :depth_t], wt[...], preferred_element_type=jnp.float32)
        teacher += jnp.dot(other[:, :depth_t], wt_beside[...], preferred_element_type=jnp.float32)
        for k in range(count):
            out[k, 0] = teacher[k * rows : (k + 1) * rows] * scales[0]
        student = jnp.dot(own[:, depth_t:], ws[...], preferred_element_type=jnp.float32)
        student += jnp.dot(other[:, depth_t:], ws_beside[...], preferred_element_type=jnp.float32)
        for k in range(count):
            out[k, 1] = student[k * rows : (k + 1) * rows] * scales[1]

    aliases = {} if buffer is None else {2 * count + 5: 0}
    more = [] if buffer is None else [pl.BlockSpec(memory_space=pltpu.HBM)]
    return pl.pallas_call(
        body,
        out_shape=jax.ShapeDtypeStruct((total, 2, rows, columns), jnp.float32),
        grid_spec=pltpu.PrefetchScalarGridSpec(
            num_scalar_prefetch=1,
            grid=(steps,),
            in_specs=[whole] * (2 * count)
            + [
                pl.BlockSpec((depth_t, tile), lambda j, core: (0, core[0] * steps + j)),
                pl.BlockSpec((depth_s, tile), lambda j, core: (0, core[0] * steps + j)),
                pl.BlockSpec((depth_t, tile), lambda j, core: (0, j)),
                pl.BlockSpec((depth_s, tile), lambda j, core: (0, j)),
            ]
            + more,
            out_specs=pl.BlockSpec((count, 2, rows, tile), lambda j, core: (start // count, 0, 0, j)),
            scratch_shapes=[pltpu.VMEM((count * rows, depth), jnp.bfloat16)] * 2,
        ),
        input_output_aliases=aliases,
        compiler_params=pltpu.CompilerParams(vmem_limit_bytes=50 * 1024 * 1024),
        cost_estimate=pl.CostEstimate(
            flops=2 * count * rows * 2 * depth * columns,
            bytes_accessed=2 * count * rows * depth * 2 + 4 * depth * columns + 2 * count * rows * columns * 4,
            transcendentals=0,
        ),
    )(core, *pieces, *others, *heads, *([] if buffer is None else [buffer]))


def unwritten(shape, dtype):
    return pl.pallas_call(
        lambda out: None,
        out_shape=jax.ShapeDtypeStruct(shape, dtype),
        out_specs=pl.BlockSpec(memory_space=pltpu.HBM),
    )()


def lookup(table, index):
    bits = max(1, max(table).bit_length())
    per = 30 // bits
    words = []
    for start in range(0, len(table), per):
        word = 0
        for k, entry in enumerate(table[start : start + per]):
            word |= entry << (k * bits)
        words.append(word)
    word = jnp.int32(words[0])
    for k in range(1, len(words)):
        word = jnp.where(index // per == k, jnp.int32(words[k]), word)
    return (word >> ((index % per) * bits)) & ((1 << bits) - 1)


def build(halves, n, toks):
    order = list(range(0, n, 2)) + list(range(n - 1, 0, -2))
    position = [order.index(v) for v in range(n)]
    owners = halves * toks
    per_owner = n // owners
    kept = n // toks
    forward = [(order[q], order[(q + 1) % n]) for q in range(n)]
    backward = [(b, a) for a, b in forward]
    swap_half = [(h, 1 - h) for h in range(halves)]
    swap_tok = [(t, 1 - t) for t in range(toks)]

    slots = [((0, 0), (0, 1))]
    for r in range(1, n // 2 + 1):
        for turn in range(2 if r < n // 2 else 1):
            slots.append(((-r, turn), (r, 1 - turn)))
    pieces = [piece for slot in slots for piece in slot]
    total = len(pieces)
    groups = groups_of(n)
    group_of = {k: g for g, group in enumerate(groups) for k in group}
    entry = [(i - 2) % total for i in range(total)]

    def ring_of(p, index):
        return (p + pieces[index][0]) % n

    def owner_of(p, index):
        return order[ring_of(p, index)] // per_owner

    away = [[[i for i in range(total) if owner_of(p, i) % toks != y] for y in range(toks)] for p in range(n)]
    exchanges = len(away[0][0])
    ready = [max(group_of[away[p][y][k] // 2] for p in range(n) for y in range(toks)) for k in range(exchanges)]

    def place_of(p, index):
        unit = order[ring_of(p, index)]
        return ((unit // per_owner) // toks * per_owner + unit % per_owner) * 2 + pieces[index][1]

    def table(value):
        return [value(p, y) for p in range(n) for y in range(toks)]

    send_index = [table(lambda p, y: entry[away[p][y][k]]) for k in range(exchanges)]
    keep_index = [table(lambda p, y: entry[away[p][1 - y][k]]) for k in range(exchanges)]
    keep_place = [table(lambda p, y: place_of(p, away[p][1 - y][k])) for k in range(exchanges)]

    def shards(teacher_hidden, student_hidden, teacher_gain, student_gain, teacher_head, student_head, labels):
        core = lax.axis_index("half")
        vocab = lax.axis_index("vocab")
        tok = lax.axis_index("tok")
        q = jnp.where(vocab % 2 == 0, vocab // 2, n - 1 - vocab // 2)
        here = q * toks + tok
        rows = teacher_hidden.shape[0]
        piece = rows // 2
        width_t = teacher_hidden.shape[1] * owners
        width_s = student_hidden.shape[1] * owners
        block = teacher_head.shape[1]
        columns = block // halves
        scales = (
            wire_scale(width_t // toks, largest_teacher),
            wire_scale(width_s // toks, largest_student),
        )

        def swap(x):
            return lax.ppermute(x, "half", swap_half)

        values_t = teacher_hidden.astype(jnp.float32)
        values_s = student_hidden.astype(jnp.float32)
        scaled = jnp.concatenate(
            [
                (values_t * teacher_gain[None, :]).astype(jnp.bfloat16),
                (values_s * student_gain[None, :]).astype(jnp.bfloat16),
            ],
            axis=1,
        )
        first, second = scaled[:piece], scaled[piece:]
        up, down = [first, second], [first, second]
        flight = {}

        def ring_step(k):
            (_, wu), (_, wd) = slots[k]
            flight[k] = (
                lax.ppermute(up[wu], "vocab", forward),
                lax.ppermute(down[wd], "vocab", backward),
            )

        ring_step(1)
        ring_step(2)

        first, second, hidden_t, hidden_s = lax.optimization_barrier(
            (first, second, teacher_hidden, student_hidden)
        )
        beside = (1 - core) * columns
        cut_t = lax.dynamic_slice_in_dim(teacher_head, beside, columns, 1)
        cut_s = lax.dynamic_slice_in_dim(student_head, beside, columns, 1)
        heads = (teacher_head, student_head, swap(cut_t), swap(cut_s))

        values_t = hidden_t.astype(jnp.float32)
        values_s = hidden_s.astype(jnp.float32)
        squares = jnp.stack([jnp.sum(values_t * values_t, axis=1), jnp.sum(values_s * values_s, axis=1)])
        squares = squares + swap(squares)
        squares = squares + lax.ppermute(squares, "tok", swap_tok)
        squares = squares[None]
        doublings = []
        reach = 1
        while reach < n:
            doublings.append(reach)
            reach *= 2

        def double_start(squares, i):
            return lax.ppermute(squares, "vocab", [(v, v ^ doublings[i]) for v in range(n)])

        def double_end(squares, near, buffer):
            near, buffer = lax.optimization_barrier((near, buffer))
            return jnp.concatenate([squares, near], axis=0), buffer

        labels_other = swap(labels)
        core_id = core.astype(jnp.int32).reshape(1)
        buffer = None
        logits = unwritten((kept * 2, 2, piece, columns), jnp.float32)
        waiting = []

        def finish(logits, buffer, k, arrived):
            mine = lax.dynamic_index_in_dim(buffer, lookup(keep_index[k], here), 0, keepdims=False)
            place = lookup(keep_place[k], here) ^ (core * per_owner * 2)
            whole = mine + arrived.astype(jnp.float32)
            return lax.dynamic_update_slice(logits, whole[None], (place, 0, 0, 0))

        def land(k, buffer):
            (_, wu), (_, wd) = slots[k]
            a, b = flight.pop(k)
            if buffer is not None:
                a, b, buffer = lax.optimization_barrier((a, b, buffer))
            up[wu], down[wd] = a, b
            if k + 2 < n:
                ring_step(k + 2)
            return [a, b], buffer

        def leave(g, buffer):
            for e in range(exchanges):
                if ready[e] == g:
                    sent = lax.dynamic_index_in_dim(buffer, lookup(send_index[e], here), 0, keepdims=False)
                    sent = sent.astype(jnp.float16)
                    buffer, sent = lax.optimization_barrier((buffer, sent))
                    waiting.append((g, e, lax.ppermute(sent, "tok", swap_tok)))
            return buffer

        for g, group in enumerate(groups):
            if g == 0:
                got = [first, second]
                near = double_start(squares, 0)
            else:
                got, buffer = land(group[0], buffer)
                buffer = leave(g - 1, buffer)
                if g < len(doublings):
                    squares, buffer = double_end(squares, near, buffer)
                    if g + 1 < len(doublings):
                        near = double_start(squares, g + 1)
                for k in group[1:]:
                    more, _ = land(k, None)
                    got += more
            start = entry[2 * group[0]]
            others = [swap(x) for x in got]
            if g == 0:
                squares, others[0] = double_end(squares, near, others[0])
                near = double_start(squares, 1)
            buffer = product(core_id, got, others, heads, scales, start, total, buffer)
        buffer = leave(len(groups) - 1, buffer)
        inverse = lax.rsqrt(
            squares / jnp.array([width_t, width_s], jnp.float32)[None, :, None] + epsilon
        ) / jnp.array(scales, jnp.float32)[None, :, None]
        inv = []
        for h in range(halves):
            for x in range(per_owner):
                unit = ((h ^ core) * toks + tok) * per_owner + x
                inv.append(lax.dynamic_index_in_dim(inverse, vocab ^ unit, 0, keepdims=False))
        inv = jnp.stack(inv).reshape(kept, 2, 2, piece)
        inv = jnp.swapaxes(inv, 1, 2).reshape(kept * 2, 2, piece)
        marks = jnp.concatenate([labels, labels_other]).reshape(kept * 2, piece)
        marks = marks - (vocab * block + core * columns)

        def local_stats(raw, factor, mark):
            teacher = raw[:, 0] * factor[:, 0, :, None]
            student = raw[:, 1] * factor[:, 1, :, None]
            max_t = jnp.max(teacher, axis=2)
            max_s = jnp.max(student, axis=2)
            exp_t = jnp.exp(teacher - max_t[:, :, None])
            exp_s = jnp.exp(student - max_s[:, :, None])
            hit = lax.broadcasted_iota(jnp.int32, teacher.shape, 2) == mark[:, :, None]
            return jnp.stack(
                [
                    max_t,
                    max_s,
                    jnp.sum(exp_t, axis=2),
                    jnp.sum(exp_t * (teacher - student), axis=2),
                    jnp.sum(exp_s, axis=2),
                    jnp.sum(jnp.where(hit, student, 0.0), axis=2),
                ]
            )

        last = len(groups) - 1
        for g, e, arrived in waiting:
            if g < last:
                logits = finish(logits, buffer, e, arrived)
        stats = local_stats(logits, inv, marks)
        logits, stats = lax.optimization_barrier((logits, stats))
        for g, e, arrived in waiting:
            if g == last:
                logits = finish(logits, buffer, e, arrived)
                place = lookup(keep_place[e], here) ^ (core * per_owner * 2)
                piece_stats = local_stats(
                    *(lax.dynamic_slice_in_dim(x, place, 1, 0) for x in (logits, inv, marks))
                )
                stats = lax.dynamic_update_slice(stats, piece_stats, (0, place, 0))
                logits, stats = lax.optimization_barrier((logits, stats))

        def merge(a, b):
            top_t = jnp.maximum(a[0], b[0])
            top_s = jnp.maximum(a[1], b[1])
            at, bt = jnp.exp(a[0] - top_t), jnp.exp(b[0] - top_t)
            as_, bs = jnp.exp(a[1] - top_s), jnp.exp(b[1] - top_s)
            return jnp.stack(
                [top_t, top_s, a[2] * at + b[2] * bt, a[3] * at + b[3] * bt, a[4] * as_ + b[4] * bs, a[5] + b[5]]
            )

        raw_theirs = (logits[kept:, 0], logits[kept:, 1])
        raw_mine = (logits[:kept, 0], logits[:kept, 1])
        stats = merge(stats, jnp.roll(swap(stats), kept, axis=1))
        reach = 1
        while reach < n:
            pairs = [(v, v ^ reach) for v in range(n)]
            beyond = lax.ppermute(stats, "vocab", pairs)
            stats = merge(stats, beyond)
            reach *= 2
        max_t, max_s, total_t, cross, total_s, target = (stats[i] for i in range(6))
        lse_t = max_t + jnp.log(total_t)
        lse_s = max_s + jnp.log(total_s)
        loss = cross / total_t - lse_t + lse_s + label_weight * (lse_s - target)
        token_loss = loss[:kept].reshape(-1)

        def gradient(part, raw):
            factor, mark, ls, lt = (x[part] for x in (inv, marks, lse_s, lse_t))
            t = raw[0] * factor[:, 0, :, None]
            s = raw[1] * factor[:, 1, :, None]
            hit = lax.broadcasted_iota(jnp.int32, t.shape, 2) == mark[:, :, None]
            grad = (
                (1.0 + label_weight) * jnp.exp(s - ls[:, :, None])
                - jnp.exp(t - lt[:, :, None])
                - label_weight * hit.astype(jnp.float32)
            )
            return grad.astype(jnp.bfloat16).reshape(-1, columns)

        theirs = gradient(slice(kept, None), raw_theirs)
        theirs, raw_mine = lax.optimization_barrier((theirs, raw_mine))
        got = swap(theirs)
        mine = gradient(slice(0, kept), raw_mine)
        logit_grad = unwritten((kept * piece, block), jnp.bfloat16)
        logit_grad = lax.dynamic_update_slice(logit_grad, mine, (0, core * columns))
        logit_grad = lax.dynamic_update_slice(logit_grad, got, (0, (1 - core) * columns))
        return (token_loss, logit_grad)

    return shards


def groups_of(n):
    return [[0]] + [[k, k + 1] for k in range(1, n - 4, 2)] + [[k] for k in range(n - 3, n)]


def solution(mesh):
    halves, n, toks = mesh.shape["half"], mesh.shape["vocab"], mesh.shape["tok"]
    return jax.shard_map(
        build(halves, n, toks),
        mesh=mesh,
        in_specs=(
            P("vocab", ("half", "tok")),
            P("vocab", ("half", "tok")),
            P(("half", "tok")),
            P(("half", "tok")),
            P(("half", "tok"), "vocab"),
            P(("half", "tok"), "vocab"),
            P(("half", "tok")),
        ),
        out_specs=(P(("half", "tok")), P(("half", "tok"), "vocab")),
        check_vma=False,
    )
```

profile of v0, /device:TPU:0, one launch (start us, length us, event | category | flops | bytes accessed | tf_op | source)
XLA Modules:
  0.0 283.5 jit_solution(18321203668519334039)
XLA Ops:
  7.5 7.4 %collective-permute-done.2 = f32[2,256]{1,0:T(2,128)S(1)} collective-permute-done((f32[2,256]{1,0:T(2,128)S(1)}, f32[2,256]{1,0:T(2,128)S(1)}, u32[]{:S(2)}, u32[]{:S(2)}) %collective-permute-start.2) | collective-permute-done | bytes 2080 | tf_op jit(solution)/shard_map/ppermute | solution.py:164
  14.9 2.9 %collective-permute-start.3 = (f32[2,256]{1,0:T(2,128)S(1)}, f32[2,256]{1,0:T(2,128)S(1)}, u32[]{:S(2)}, u32[]{:S(2)}) collective-permute-start(f32[2,256]{1,0:T(2,128)S(1)} %fusion.92), channel_id=1, source_target_pairs={{0,1},{1,0},{2,3},{3,2},{4,5},{5,4},{6,7},{7,6},{8,9},{9,8},{10,11... | collective-permute-start | bytes 6152 | tf_op jit(solution)/shard_map/ppermute | solution.py:201
  27.2 16.3 %collective-permute-done.refs_0_ = bf16[128,3072]{1,0:T(8,128)(2,1)S(1)} collective-permute-done((bf16[128,3072]{1,0:T(8,128)(2,1)S(1)}, bf16[128,3072]{1,0:T(8,128)(2,1)S(1)}, u32[]{:S(2)}, u32[]{:S(2)}) %collective-permute-start) | collective-permute-done | bytes 786464 | tf_op jit(solution)/shard_map/ppermute | solution.py:182
  45.5 12.0 %collective-permute-done.11.refs_2_ = bf16[128,3072]{1,0:T(8,128)(2,1)S(1)} collective-permute-done((bf16[128,3072]{1,0:T(8,128)(2,1)S(1)}, bf16[128,3072]{1,0:T(8,128)(2,1)S(1)}, u32[]{:S(2)}, u32[]{:S(2)}) %collective-permute-start.11) | collective-permute-done | bytes 786464 | tf_op jit(solution)/shard_map/ppermute | solution.py:182
  62.1 7.7 %shard_map.105.refs_12_ = f32[16,2,128,1024]{3,2,1,0:T(8,128)} custom-call(s32[1]{0:T(128)} %bitcast.core, bf16[128,3072]{1,0:T(8,128)(2,1)S(1)} %get-tuple-element.52.refs_0_, bf16[128,3072]{1,0:T(8,128)(2,1)S(1)} %get-tuple-element.53.refs_1_, bf16[128,3072]{1,0:T(8,128)(2,1)S(1)} %collective-permute-done.5.refs_2_, ...), custom_call_target="tpu_custom_call" | custom-call | flops 3221225472 | bytes 17825792 | tf_op jit(solution)/shard_map/pallas_call | solution.py:54
  73.2 5.8 %collective-permute-done.20.refs_2_ = bf16[128,3072]{1,0:T(8,128)(2,1)S(1)} collective-permute-done((bf16[128,3072]{1,0:T(8,128)(2,1)S(1)}, bf16[128,3072]{1,0:T(8,128)(2,1)S(1)}, u32[]{:S(2)}, u32[]{:S(2)}) %collective-permute-start.20) | collective-permute-done | bytes 786464 | tf_op jit(solution)/shard_map/ppermute | solution.py:182
  79.7 11.0 %collective-permute-done.21.refs_3_ = bf16[128,3072]{1,0:T(8,128)(2,1)S(1)} collective-permute-done((bf16[128,3072]{1,0:T(8,128)(2,1)S(1)}, bf16[128,3072]{1,0:T(8,128)(2,1)S(1)}, u32[]{:S(2)}, u32[]{:S(2)}) %collective-permute-start.21) | collective-permute-done | bytes 786464 | tf_op jit(solution)/shard_map/ppermute | solution.py:183
  92.1 12.0 %shard_map.106.refs_12_ = f32[16,2,128,1024]{3,2,1,0:T(8,128)} custom-call(s32[1]{0:T(128)} %bitcast.core, bf16[128,3072]{1,0:T(8,128)(2,1)S(1)} %collective-permute-done.refs_0_, bf16[128,3072]{1,0:T(8,128)(2,1)S(1)} %collective-permute-done.1.refs_1_, bf16[128,3072]{1,0:T(8,128)(2,1)S(1)} %collective-permute-done.11.refs_2_, ...), custom_call_target="tpu_custom_call", output_to_operand_aliasing={{}: (13, {})} | custom-call | flops 6442450944 | bytes 23068672 | tf_op jit(solution)/shard_map/pallas_call | solution.py:54
  107.3 3.0 %collective-permute-done.43 = s32[512]{0:T(512)S(1)} collective-permute-done((s32[512]{0:T(512)S(1)}, s32[512]{0:T(512)S(1)}, u32[]{:S(2)}, u32[]{:S(2)}) %collective-permute-start.43) | collective-permute-done | bytes 2080 | tf_op jit(solution)/shard_map/ppermute | solution.py:164
  120.2 12.3 %shard_map.107.refs_8_ = f32[16,2,128,1024]{3,2,1,0:T(8,128)} custom-call(s32[1]{0:T(128)} %bitcast.core, bf16[128,3072]{1,0:T(8,128)(2,1)S(1)} %collective-permute-done.9.refs_0_, bf16[128,3072]{1,0:T(8,128)(2,1)S(1)} %collective-permute-done.10.refs_1_, bf16[128,3072]{1,0:T(8,128)(2,1)S(1)} %collective-permute-done.20.refs_2_, ...), custom_call_target="tpu_custom_call", output_to_operand_aliasing={{}: (13, {})} | custom-call | flops 6442450944 | bytes 23068672 | tf_op jit(solution)/shard_map/pallas_call | solution.py:54
  141.7 7.6 %shard_map.108.refs_8_ = f32[16,2,128,1024]{3,2,1,0:T(8,128)} custom-call(s32[1]{0:T(128)} %bitcast.core, bf16[128,3072]{1,0:T(8,128)(2,1)S(1)} %collective-permute-done.18.refs_0_, bf16[128,3072]{1,0:T(8,128)(2,1)S(1)} %collective-permute-done.19.refs_1_, bf16[128,3072]{1,0:T(8,128)(2,1)S(1)} %collective-permute-done.31.refs_2_, ...), custom_call_target="tpu_custom_call", output_to_operand_aliasing={{}: (9, {})} | custom-call | flops 3221225472 | bytes 17825792 | tf_op jit(solution)/shard_map/pallas_call | solution.py:54
  149.4 3.9 %collective-permute-done.29.refs_0_ = bf16[128,3072]{1,0:T(8,128)(2,1)S(1)} collective-permute-done((bf16[128,3072]{1,0:T(8,128)(2,1)S(1)}, bf16[128,3072]{1,0:T(8,128)(2,1)S(1)}, u32[]{:S(2)}, u32[]{:S(2)}) %collective-permute-start.29) | collective-permute-done | bytes 786464 | tf_op jit(solution)/shard_map/ppermute | solution.py:182
  161.2 7.7 %shard_map.109.refs_8_ = f32[16,2,128,1024]{3,2,1,0:T(8,128)} custom-call(s32[1]{0:T(128)} %bitcast.core, bf16[128,3072]{1,0:T(8,128)(2,1)S(1)} %collective-permute-done.29.refs_0_, bf16[128,3072]{1,0:T(8,128)(2,1)S(1)} %collective-permute-done.30.refs_1_, bf16[128,3072]{1,0:T(8,128)(2,1)S(1)} %collective-permute-done.33.refs_2_, ...), custom_call_target="tpu_custom_call", output_to_operand_aliasing={{}: (9, {})} | custom-call | flops 3221225472 | bytes 17825792 | tf_op jit(solution)/shard_map/pallas_call | solution.py:54
  168.9 6.1 %collective-permute-done.27.refs_0_ = bf16[128,3072]{1,0:T(8,128)(2,1)S(1)} collective-permute-done((bf16[128,3072]{1,0:T(8,128)(2,1)S(1)}, bf16[128,3072]{1,0:T(8,128)(2,1)S(1)}, u32[]{:S(2)}, u32[]{:S(2)}) %collective-permute-start.27) | collective-permute-done | bytes 786464 | tf_op jit(solution)/shard_map/ppermute | solution.py:182
  182.1 7.6 %shard_map.110 = f32[16,2,128,1024]{3,2,1,0:T(8,128)} custom-call(s32[1]{0:T(128)} %bitcast.core, bf16[128,3072]{1,0:T(8,128)(2,1)S(1)} %collective-permute-done.27.refs_0_, bf16[128,3072]{1,0:T(8,128)(2,1)S(1)} %collective-permute-done.28.refs_1_, bf16[128,3072]{1,0:T(8,128)(2,1)S(1)} %collective-permute-done.35.refs_2_, ...), custom_call_target="tpu_custom_call", output_to_operand_aliasing={{}: (9, {})} | custom-call | flops 3221225472 | bytes 17825792 | tf_op jit(solution)/shard_map/pallas_call | solution.py:54
  198.0 4.7 %collective-permute-done.40 = f16[2,128,1024]{2,1,0:T(8,128)(2,1)} collective-permute-done((f16[2,128,1024]{2,1,0:T(8,128)(2,1)}, f16[2,128,1024]{2,1,0:T(8,128)(2,1)}, u32[]{:S(2)}, u32[]{:S(2)}) %collective-permute-start.40) | collective-permute-done | bytes 524320 | tf_op jit(solution)/shard_map/ppermute | solution.py:244
  204.3 9.5 %collective-permute-done.41 = f16[2,128,1024]{2,1,0:T(8,128)(2,1)S(1)} collective-permute-done((f16[2,128,1024]{2,1,0:T(8,128)(2,1)}, f16[2,128,1024]{2,1,0:T(8,128)(2,1)S(1)}, u32[]{:S(2)}, u32[]{:S(2)}) %collective-permute-start.41) | collective-permute-done | bytes 524320 | tf_op jit(solution)/shard_map/ppermute | solution.py:244
  215.2 8.8 %collective-permute-done.42 = f16[2,128,1024]{2,1,0:T(8,128)(2,1)S(1)} collective-permute-done((f16[2,128,1024]{2,1,0:T(8,128)(2,1)}, f16[2,128,1024]{2,1,0:T(8,128)(2,1)S(1)}, u32[]{:S(2)}, u32[]{:S(2)}) %collective-permute-start.42) | collective-permute-done | bytes 524320 | tf_op jit(solution)/shard_map/ppermute | solution.py:244
  226.5 3.2 %select_reduce_fusion = (f32[8,128]{1,0:T(8,128)S(1)}, f32[8,128]{1,0:T(8,128)S(1)}, f32[8,128]{1,0:T(8,128)S(1)}, f32[8,128]{1,0:T(8,128)S(1)}) fusion(f32[8,2,128,1024]{3,2,1,0:T(8,128)S(1)} %bitcast_dynamic-update-slice_fusion.2, s32[8,128]{1,0:T(8,128)S(1)} %add_subtract_fusion, f32[8,128]{1,0:T(8,128)S(1)} %bitcast.545, ...), kind=kLoop, calls=%fused_computation.4 | loop fusion | flops 12578816 | bytes 8425472 | tf_op jit(solution)/shard_map/reduce_sum | solution.py:296
  231.9 12.7 %collective-permute-done.44 = f16[2,128,1024]{2,1,0:T(8,128)(2,1)S(1)} collective-permute-done((f16[2,128,1024]{2,1,0:T(8,128)(2,1)S(1)}, f16[2,128,1024]{2,1,0:T(8,128)(2,1)S(1)}, u32[]{:S(2)}, u32[]{:S(2)}) %collective-permute-start.44) | collective-permute-done | bytes 524320 | tf_op jit(solution)/shard_map/ppermute | solution.py:244
  246.2 3.0 %copy-done.1 = f32[8,2,128,1024]{3,2,1,0:T(8,128)} copy-done((f32[8,2,128,1024]{3,2,1,0:T(8,128)}, f32[8,2,128,1024]{3,2,1,0:T(8,128)S(1)}, u32[]{:S(2)}) %copy-start.1) | copy-done | bytes 8388632
  249.8 4.2 %collective-permute-done.45 = f16[2,128,1024]{2,1,0:T(8,128)(2,1)S(1)} collective-permute-done((f16[2,128,1024]{2,1,0:T(8,128)(2,1)}, f16[2,128,1024]{2,1,0:T(8,128)(2,1)S(1)}, u32[]{:S(2)}, u32[]{:S(2)}) %collective-permute-start.45) | collective-permute-done | bytes 524320 | tf_op jit(solution)/shard_map/ppermute | solution.py:244
  262.0 2.9 %collective-permute-done.47 = f32[6,8,128]{2,1,0:T(8,128)S(1)} collective-permute-done((f32[6,8,128]{2,1,0:T(8,128)S(1)}, f32[6,8,128]{2,1,0:T(8,128)S(1)}, u32[]{:S(2)}, u32[]{:S(2)}) %collective-permute-start.47) | collective-permute-done | bytes 24608 | tf_op jit(solution)/shard_map/ppermute | solution.py:331
  265.9 5.0 %slice_bitcast_fusion.3 = (f32[4,128,1024]{2,1,0:T(8,128)}, f32[4,1,128,1024]{3,2,1,0:T(8,128)S(1)}, f32[4,1,128,1024]{3,2,1,0:T(8,128)S(1)}) fusion(f32[8,2,128,1024]{3,2,1,0:T(8,128)} %bitcast_dynamic-update-slice_fusion), kind=kLoop, calls=%fused_computation.25 | loop fusion | bytes 12582912 | tf_op jit(solution)/shard_map/squeeze | solution.py:326
  (215 shorter events, 104.8 us)
Async XLA Ops:
  3.4 56.2 %collective-permute-start.7 = (bf16[2048,1024]{1,0:T(8,128)(2,1)S(1)}, bf16[2048,1024]{1,0:T(8,128)(2,1)S(1)}, u32[]{:S(2)}, u32[]{:S(2)}) collective-permute-start(bf16[2048,1024]{1,0:T(8,128)(2,1)S(1)} %constant_dynamic-slice_fusion.9), channel_id=1, source_target_pairs={{0,16},{16,0},{1,17},{17,1},{2,18},{18,2},{3,19},{19,3},{4,20},{20... | collective-permute-start | bytes 12582920 | tf_op jit(solution)/shard_map/ppermute | solution.py:164
  4.5 20.7 %collective-permute-start.5 = (bf16[128,3072]{1,0:T(8,128)(2,1)S(1)}, bf16[128,3072]{1,0:T(8,128)(2,1)S(1)}, u32[]{:S(2)}, u32[]{:S(2)}) collective-permute-start(bf16[128,3072]{1,0:T(8,128)(2,1)S(1)} %get-tuple-element.52.refs_0_), channel_id=1, source_target_pairs={{0,16},{16,0},{1,17},{17,1},{2,18},{18,2},{3,19},{19,3},{4,20},{20... | collective-permute-start | bytes 2359304 | tf_op jit(solution)/shard_map/ppermute | solution.py:164
  5.9 53.5 %collective-permute-start.8 = (bf16[1024,1024]{1,0:T(8,128)(2,1)S(1)}, bf16[1024,1024]{1,0:T(8,128)(2,1)S(1)}, u32[]{:S(2)}, u32[]{:S(2)}) collective-permute-start(bf16[1024,1024]{1,0:T(8,128)(2,1)S(1)} %constant_dynamic-slice_fusion.8), channel_id=1, source_target_pairs={{0,16},{16,0},{1,17},{17,1},{2,18},{18,2},{3,19},{19,3},{4,20},{20... | collective-permute-start | bytes 6291464 | tf_op jit(solution)/shard_map/ppermute | solution.py:164
  7.0 19.8 %collective-permute-start.6 = (bf16[128,3072]{1,0:T(8,128)(2,1)S(1)}, bf16[128,3072]{1,0:T(8,128)(2,1)S(1)}, u32[]{:S(2)}, u32[]{:S(2)}) collective-permute-start(bf16[128,3072]{1,0:T(8,128)(2,1)S(1)} %get-tuple-element.53.refs_1_), channel_id=1, source_target_pairs={{0,16},{16,0},{1,17},{17,1},{2,18},{18,2},{3,19},{19,3},{4,20},{20... | collective-permute-start | bytes 2359304 | tf_op jit(solution)/shard_map/ppermute | solution.py:164
  23.1 20.4 %collective-permute-start = (bf16[128,3072]{1,0:T(8,128)(2,1)S(1)}, bf16[128,3072]{1,0:T(8,128)(2,1)S(1)}, u32[]{:S(2)}, u32[]{:S(2)}) collective-permute-start(bf16[128,3072]{1,0:T(8,128)(2,1)S(1)} %get-tuple-element.52.refs_0_), channel_id=1, source_target_pairs={{0,4},{4,8},{8,12},{12,14},{14,10},{10,6},{6,2},{2,0},{1,5},{5,9},... | collective-permute-start | bytes 2359304 | tf_op jit(solution)/shard_map/ppermute | solution.py:182
  25.2 32.3 %collective-permute-start.11 = (bf16[128,3072]{1,0:T(8,128)(2,1)S(1)}, bf16[128,3072]{1,0:T(8,128)(2,1)S(1)}, u32[]{:S(2)}, u32[]{:S(2)}) collective-permute-start(bf16[128,3072]{1,0:T(8,128)(2,1)S(1)} %get-tuple-element.53.refs_1_), channel_id=1, source_target_pairs={{0,4},{4,8},{8,12},{12,14},{14,10},{10,6},{6,2},{2,0},{1,5},{5,9},... | collective-permute-start | bytes 2359304 | tf_op jit(solution)/shard_map/ppermute | solution.py:182
  26.8 30.7 %collective-permute-start.12 = (bf16[128,3072]{1,0:T(8,128)(2,1)S(1)}, bf16[128,3072]{1,0:T(8,128)(2,1)S(1)}, u32[]{:S(2)}, u32[]{:S(2)}) collective-permute-start(bf16[128,3072]{1,0:T(8,128)(2,1)S(1)} %get-tuple-element.52.refs_0_), channel_id=1, source_target_pairs={{4,0},{8,4},{12,8},{14,12},{10,14},{6,10},{2,6},{0,2},{5,1},{9,5},... | collective-permute-start | bytes 2359304 | tf_op jit(solution)/shard_map/ppermute | solution.py:183
  43.5 26.3 %collective-permute-start.1 = (bf16[128,3072]{1,0:T(8,128)(2,1)S(1)}, bf16[128,3072]{1,0:T(8,128)(2,1)S(1)}, u32[]{:S(2)}, u32[]{:S(2)}) collective-permute-start(bf16[128,3072]{1,0:T(8,128)(2,1)S(1)} %get-tuple-element.53.refs_1_), channel_id=1, source_target_pairs={{4,0},{8,4},{12,8},{14,12},{10,14},{6,10},{2,6},{0,2},{5,1},{9,5},... | collective-permute-start | bytes 2359304 | tf_op jit(solution)/shard_map/ppermute | solution.py:183
  59.4 19.7 %collective-permute-start.20 = (bf16[128,3072]{1,0:T(8,128)(2,1)S(1)}, bf16[128,3072]{1,0:T(8,128)(2,1)S(1)}, u32[]{:S(2)}, u32[]{:S(2)}) collective-permute-start(bf16[128,3072]{1,0:T(8,128)(2,1)S(1)} %collective-permute-done.11.refs_2_), channel_id=1, source_target_pairs={{0,4},{4,8},{8,12},{12,14},{14,10},{10,6},{6,2},{2,0},{1,5},{5,9},... | collective-permute-start | bytes 2359304 | tf_op jit(solution)/shard_map/ppermute | solution.py:182
  69.8 20.9 %collective-permute-start.21 = (bf16[128,3072]{1,0:T(8,128)(2,1)S(1)}, bf16[128,3072]{1,0:T(8,128)(2,1)S(1)}, u32[]{:S(2)}, u32[]{:S(2)}) collective-permute-start(bf16[128,3072]{1,0:T(8,128)(2,1)S(1)} %collective-permute-done.12.refs_3_), channel_id=1, source_target_pairs={{4,0},{8,4},{12,8},{14,12},{10,14},{6,10},{2,6},{0,2},{5,1},{9,5},... | collective-permute-start | bytes 2359304 | tf_op jit(solution)/shard_map/ppermute | solution.py:183
  71.3 19.9 %collective-permute-start.14 = (bf16[128,3072]{1,0:T(8,128)(2,1)S(1)}, bf16[128,3072]{1,0:T(8,128)(2,1)S(1)}, u32[]{:S(2)}, u32[]{:S(2)}) collective-permute-start(bf16[128,3072]{1,0:T(8,128)(2,1)S(1)} %collective-permute-done.1.refs_1_), channel_id=1, source_target_pairs={{0,16},{16,0},{1,17},{17,1},{2,18},{18,2},{3,19},{19,3},{4,20},{20... | collective-permute-start | bytes 2359304 | tf_op jit(solution)/shard_map/ppermute | solution.py:164
  71.8 34.9 %collective-permute-start.10 = (bf16[128,3072]{1,0:T(8,128)(2,1)S(1)}, bf16[128,3072]{1,0:T(8,128)(2,1)S(1)}, u32[]{:S(2)}, u32[]{:S(2)}) collective-permute-start(bf16[128,3072]{1,0:T(8,128)(2,1)S(1)} %collective-permute-done.1.refs_1_), channel_id=1, source_target_pairs={{4,0},{8,4},{12,8},{14,12},{10,14},{6,10},{2,6},{0,2},{5,1},{9,5},... | collective-permute-start | bytes 2359304 | tf_op jit(solution)/shard_map/ppermute | solution.py:183
  79.0 27.8 %collective-permute-start.9 = (bf16[128,3072]{1,0:T(8,128)(2,1)S(1)}, bf16[128,3072]{1,0:T(8,128)(2,1)S(1)}, u32[]{:S(2)}, u32[]{:S(2)}) collective-permute-start(bf16[128,3072]{1,0:T(8,128)(2,1)S(1)} %collective-permute-done.refs_0_), channel_id=1, source_target_pairs={{0,4},{4,8},{8,12},{12,14},{14,10},{10,6},{6,2},{2,0},{1,5},{5,9},... | collective-permute-start | bytes 2359304 | tf_op jit(solution)/shard_map/ppermute | solution.py:182
  90.7 21.8 %collective-permute-start.24 = (bf16[128,3072]{1,0:T(8,128)(2,1)S(1)}, bf16[128,3072]{1,0:T(8,128)(2,1)}, u32[]{:S(2)}, u32[]{:S(2)}) collective-permute-start(bf16[128,3072]{1,0:T(8,128)(2,1)S(1)} %collective-permute-done.20.refs_2_), channel_id=1, source_target_pairs={{0,16},{16,0},{1,17},{17,1},{2,18},{18,2},{3,19},{19,3},{4,20},{20... | collective-permute-start | bytes 2359304 | tf_op jit(solution)/shard_map/ppermute | solution.py:164
  90.7 29.5 %collective-permute-start.25 = (bf16[128,3072]{1,0:T(8,128)(2,1)S(1)}, bf16[128,3072]{1,0:T(8,128)(2,1)}, u32[]{:S(2)}, u32[]{:S(2)}) collective-permute-start(bf16[128,3072]{1,0:T(8,128)(2,1)S(1)} %collective-permute-done.21.refs_3_), channel_id=1, source_target_pairs={{0,16},{16,0},{1,17},{17,1},{2,18},{18,2},{3,19},{19,3},{4,20},{20... | collective-permute-start | bytes 2359304 | tf_op jit(solution)/shard_map/ppermute | solution.py:164
  112.5 20.1 %collective-permute-start.18 = (bf16[128,3072]{1,0:T(8,128)(2,1)S(1)}, bf16[128,3072]{1,0:T(8,128)(2,1)S(1)}, u32[]{:S(2)}, u32[]{:S(2)}) collective-permute-start(bf16[128,3072]{1,0:T(8,128)(2,1)S(1)} %collective-permute-done.9.refs_0_), channel_id=1, source_target_pairs={{0,4},{4,8},{8,12},{12,14},{14,10},{10,6},{6,2},{2,0},{1,5},{5,9},... | collective-permute-start | bytes 2359304 | tf_op jit(solution)/shard_map/ppermute | solution.py:182
  135.9 57.3 %collective-permute-start.37 = (f16[2,128,1024]{2,1,0:T(8,128)(2,1)}, f16[2,128,1024]{2,1,0:T(8,128)(2,1)S(1)}, u32[]{:S(2)}, u32[]{:S(2)}) collective-permute-start(f16[2,128,1024]{2,1,0:T(8,128)(2,1)} %fusion.14), channel_id=1, source_target_pairs={{0,1},{1,0},{2,3},{3,2},{4,5},{5,4},{6,7},{7,6},{8,9},{9,8},{10,11... | collective-permute-start | bytes 1572872 | tf_op jit(solution)/shard_map/ppermute | solution.py:244
  155.3 19.7 %collective-permute-start.27 = (bf16[128,3072]{1,0:T(8,128)(2,1)S(1)}, bf16[128,3072]{1,0:T(8,128)(2,1)S(1)}, u32[]{:S(2)}, u32[]{:S(2)}) collective-permute-start(bf16[128,3072]{1,0:T(8,128)(2,1)S(1)} %collective-permute-done.18.refs_0_), channel_id=1, source_target_pairs={{0,4},{4,8},{8,12},{12,14},{14,10},{10,6},{6,2},{2,0},{1,5},{5,9},... | collective-permute-start | bytes 2359304 | tf_op jit(solution)/shard_map/ppermute | solution.py:182
  159.7 35.4 %collective-permute-start.38 = (f16[2,128,1024]{2,1,0:T(8,128)(2,1)}, f16[2,128,1024]{2,1,0:T(8,128)(2,1)S(1)}, u32[]{:S(2)}, u32[]{:S(2)}) collective-permute-start(f16[2,128,1024]{2,1,0:T(8,128)(2,1)} %fusion.15), channel_id=1, source_target_pairs={{0,1},{1,0},{2,3},{3,2},{4,5},{5,4},{6,7},{7,6},{8,9},{9,8},{10,11... | collective-permute-start | bytes 1572872 | tf_op jit(solution)/shard_map/ppermute | solution.py:244
  176.3 20.3 %collective-permute-start.39 = (f16[2,128,1024]{2,1,0:T(8,128)(2,1)}, f16[2,128,1024]{2,1,0:T(8,128)(2,1)S(1)}, u32[]{:S(2)}, u32[]{:S(2)}) collective-permute-start(f16[2,128,1024]{2,1,0:T(8,128)(2,1)} %fusion.16), channel_id=1, source_target_pairs={{0,1},{1,0},{2,3},{3,2},{4,5},{5,4},{6,7},{7,6},{8,9},{9,8},{10,11... | collective-permute-start | bytes 1572872 | tf_op jit(solution)/shard_map/ppermute | solution.py:244
  180.1 22.6 %collective-permute-start.40 = (f16[2,128,1024]{2,1,0:T(8,128)(2,1)}, f16[2,128,1024]{2,1,0:T(8,128)(2,1)}, u32[]{:S(2)}, u32[]{:S(2)}) collective-permute-start(f16[2,128,1024]{2,1,0:T(8,128)(2,1)} %fusion.17), channel_id=1, source_target_pairs={{0,1},{1,0},{2,3},{3,2},{4,5},{5,4},{6,7},{7,6},{8,9},{9,8},{10,11... | collective-permute-start | bytes 1572872 | tf_op jit(solution)/shard_map/ppermute | solution.py:244
  180.6 33.2 %collective-permute-start.41 = (f16[2,128,1024]{2,1,0:T(8,128)(2,1)}, f16[2,128,1024]{2,1,0:T(8,128)(2,1)S(1)}, u32[]{:S(2)}, u32[]{:S(2)}) collective-permute-start(f16[2,128,1024]{2,1,0:T(8,128)(2,1)} %fusion.18), channel_id=1, source_target_pairs={{0,1},{1,0},{2,3},{3,2},{4,5},{5,4},{6,7},{7,6},{8,9},{9,8},{10,11... | collective-permute-start | bytes 1572872 | tf_op jit(solution)/shard_map/ppermute | solution.py:244
  193.2 30.9 %collective-permute-start.42 = (f16[2,128,1024]{2,1,0:T(8,128)(2,1)}, f16[2,128,1024]{2,1,0:T(8,128)(2,1)S(1)}, u32[]{:S(2)}, u32[]{:S(2)}) collective-permute-start(f16[2,128,1024]{2,1,0:T(8,128)(2,1)} %fusion.19), channel_id=1, source_target_pairs={{0,1},{1,0},{2,3},{3,2},{4,5},{5,4},{6,7},{7,6},{8,9},{9,8},{10,11... | collective-permute-start | bytes 1572872 | tf_op jit(solution)/shard_map/ppermute | solution.py:244
  231.3 22.7 %collective-permute-start.45 = (f16[2,128,1024]{2,1,0:T(8,128)(2,1)}, f16[2,128,1024]{2,1,0:T(8,128)(2,1)S(1)}, u32[]{:S(2)}, u32[]{:S(2)}) collective-permute-start(f16[2,128,1024]{2,1,0:T(8,128)(2,1)} %fusion.21), channel_id=1, source_target_pairs={{0,1},{1,0},{2,3},{3,2},{4,5},{5,4},{6,7},{7,6},{8,9},{9,8},{10,11... | collective-permute-start | bytes 1572872 | tf_op jit(solution)/shard_map/ppermute | solution.py:244
  (42 other events, 369.5 us)
where the time goes:
time: 284 us; the launch traced here: 283 us
  waiting for transfers between devices  121 us (43%)
  Pallas kernels  55 us (19%)
  starting transfers between devices  43.5 us (15%)
  other arithmetic  42.1 us (15%)
  local copies, waits for them, and re-layouts  20.8 us (7%)
    pallas_call x6, Pallas kernels, product(): pl.pallas_call(body, out_shape=jax.ShapeDtypeStruct((total, 2, rows, colu...  55 us
    ppermute x7, waiting for transfers between devices, ring_step(): lax.ppermute(up[wu], 'vocab', forward)  44.1 us
    ppermute x8, waiting for transfers between devices, leave(): waiting.append((g, e, lax.ppermute(sent, 'tok', swap_tok)))  39.9 us
    ppermute x7, waiting for transfers between devices, ring_step(): lax.ppermute(down[wd], 'vocab', backward)  16.7 us
    convert_element_type x8, other arithmetic, leave(): sent = sent.astype(jnp.float16)  16.2 us
    dynamic_update_slice x8, other arithmetic, finish(): return lax.dynamic_update_slice(logits, whole[None], (place, 0, 0, 0))  12.7 us
    ppermute x22, waiting for transfers between devices, swap(): return lax.ppermute(x, 'half', swap_half)  11.7 us
    ppermute x8, starting transfers between devices, leave(): waiting.append((g, e, lax.ppermute(sent, 'tok', swap_tok)))  9.31 us
  transfers between devices with their start and end apart: 51, of which 23 were waited for; matrix products, arithmetic and copies ran while one was open for 13% of the time, Pallas kernels for 19%

commit v1 on v0

--- a/solution.py
+++ b/solution.py
@@ -198,7 +198,9 @@
         values_s = hidden_s.astype(jnp.float32)
         squares = jnp.stack([jnp.sum(values_t * values_t, axis=1), jnp.sum(values_s * values_s, axis=1)])
         squares = squares + swap(squares)
+        labels_other = swap(labels)
         squares = squares + lax.ppermute(squares, "tok", swap_tok)
+        squares, labels_other = lax.optimization_barrier((squares, labels_other))
         squares = squares[None]
         doublings = []
         reach = 1
@@ -213,7 +215,6 @@
             near, buffer = lax.optimization_barrier((near, buffer))
             return jnp.concatenate([squares, near], axis=0), buffer
 
-        labels_other = swap(labels)
         core_id = core.astype(jnp.int32).reshape(1)
         buffer = None
         logits = unwritten((kept * 2, 2, piece, columns), jnp.float32)
@@ -233,7 +234,7 @@
             up[wu], down[wd] = a, b
             if k + 2 < n:
                 ring_step(k + 2)
-            return [a, b], buffer
+            return [a, b], [swap(a), swap(b)], buffer
 
         def leave(g, buffer):
             for e in range(exchanges):
@@ -248,18 +249,20 @@
             if g == 0:
                 got = [first, second]
                 near = double_start(squares, 0)
+                others = [swap(first), swap(second)]
             else:
-                got, buffer = land(group[0], buffer)
+                got, others, buffer = land(group[0], buffer)
                 buffer = leave(g - 1, buffer)
-                if g < len(doublings):
+                step = (g + 1) // 2
+                if g % 2 == 1 and step < len(doublings):
                     squares, buffer = double_end(squares, near, buffer)
-                    if g + 1 < len(doublings):
-                        near = double_start(squares, g + 1)
+                    if step + 1 < len(doublings):
+                        near = double_start(squares, step + 1)
                 for k in group[1:]:
-                    more, _ = land(k, None)
+                    more, beside_more, _ = land(k, None)
                     got += more
+                    others += beside_more
             start = entry[2 * group[0]]
-            others = [swap(x) for x in got]
             if g == 0:
                 squares, others[0] = double_end(squares, near, others[0])
                 near = double_start(squares, 1)
@@ -362,7 +365,7 @@
 
 
 def groups_of(n):
-    return [[0]] + [[k, k + 1] for k in range(1, n - 4, 2)] + [[k] for k in range(n - 3, n)]
+    return [[k] for k in range(n)]
 
 
 def solution(mesh):

time: 284 us -> 296 us (1.042)
  Pallas kernels: 55 us -> 65 us
  waiting for transfers between devices: 121 us -> 126 us
    ppermute x3, waiting for transfers between devices: 2.96 us -> 34.2 us  [double_start(): lax.ppermute(squares, 'vocab', [(v, v ^ doublings[i]) for v in range(n)])]
    ppermute x7, waiting for transfers between devices: 16.7 us -> 4.11 us  [ring_step(): lax.ppermute(down[wd], 'vocab', backward)]
    ppermute x7, waiting for transfers between devices: 44.1 us -> 32.1 us  [ring_step(): lax.ppermute(up[wu], 'vocab', forward)]
    pallas_call x6 -> x8, Pallas kernels: 55 us -> 65 us  [product(): pl.pallas_call(body, out_shape=jax.ShapeDtypeStruct((total, 2, rows, colu...]
    unnamed x45 -> x43, local copies, waits for them, and re-layouts: 8.84 us -> 7.21 us
  transfers between devices with their start and end apart: 51 -> 51, of which waited for: 23 -> 24; matrix products, arithmetic and copies ran while one was open for 13% -> 13% of each run, Pallas kernels for 19% -> 22%
where the time goes in v1:
time: 296 us; the launch traced here: 295 us
  waiting for transfers between devices  126 us (43%)
  Pallas kernels  65 us (22%)
  other arithmetic  42 us (14%)
  starting transfers between devices  41.4 us (14%)
  local copies, waits for them, and re-layouts  19.4 us (7%)
    pallas_call x8, Pallas kernels, product(): pl.pallas_call(body, out_shape=jax.ShapeDtypeStruct((total, 2, rows, colu...  65 us
    ppermute x8, waiting for transfers between devices, leave(): waiting.append((g, e, lax.ppermute(sent, 'tok', swap_tok)))  40 us
    ppermute x3, waiting for transfers between devices, double_start(): lax.ppermute(squares, 'vocab', [(v, v ^ doublings[i]) for v in range(n)])  34.2 us
    ppermute x7, waiting for transfers between devices, ring_step(): lax.ppermute(up[wu], 'vocab', forward)  32.1 us
    convert_element_type x8, other arithmetic, leave(): sent = sent.astype(jnp.float16)  16.2 us
    dynamic_update_slice x8, other arithmetic, finish(): return lax.dynamic_update_slice(logits, whole[None], (place, 0, 0, 0))  12.5 us
    ppermute x22, waiting for transfers between devices, swap(): return lax.ppermute(x, 'half', swap_half)  10.4 us
    ppermute x8, starting transfers between devices, leave(): waiting.append((g, e, lax.ppermute(sent, 'tok', swap_tok)))  9.38 us
  transfers between devices with their start and end apart: 51, of which 24 were waited for; matrix products, arithmetic and copies ran while one was open for 13% of the time, Pallas kernels for 22%

profile of v1, /device:TPU:0, one launch (start us, length us, event | category | flops | bytes accessed | tf_op | source)
XLA Modules:
  0.0 295.2 jit_solution(2945435527246712592)
XLA Ops:
  6.9 8.0 %collective-permute-done.2 = f32[2,256]{1,0:T(2,128)S(1)} collective-permute-done((f32[2,256]{1,0:T(2,128)S(1)}, f32[2,256]{1,0:T(2,128)S(1)}, u32[]{:S(2)}, u32[]{:S(2)}) %collective-permute-start.2) | collective-permute-done | bytes 2080 | tf_op jit(solution)/shard_map/ppermute | solution.py:164
  29.1 7.7 %shard_map.105.refs_8_ = f32[16,2,128,1024]{3,2,1,0:T(8,128)} custom-call(s32[1]{0:T(128)} %bitcast.core, bf16[128,3072]{1,0:T(8,128)(2,1)S(1)} %get-tuple-element.60.refs_0_, bf16[128,3072]{1,0:T(8,128)(2,1)S(1)} %get-tuple-element.61.refs_1_, bf16[128,3072]{1,0:T(8,128)(2,1)S(1)} %collective-permute-done.6.refs_2_, ...), custom_call_target="tpu_custom_call" | custom-call | flops 3221225472 | bytes 17825792 | tf_op jit(solution)/shard_map/pallas_call | solution.py:54
  36.7 6.3 %collective-permute-done.refs_0_ = bf16[128,3072]{1,0:T(8,128)(2,1)} collective-permute-done((bf16[128,3072]{1,0:T(8,128)(2,1)S(1)}, bf16[128,3072]{1,0:T(8,128)(2,1)}, u32[]{:S(2)}, u32[]{:S(2)}) %collective-permute-start) | collective-permute-done | bytes 786464 | tf_op jit(solution)/shard_map/ppermute | solution.py:182
  48.7 17.2 %collective-permute-done.16 = f32[2,2,256]{2,1,0:T(2,128)S(1)} collective-permute-done((f32[2,2,256]{2,1,0:T(2,128)S(1)}, f32[2,2,256]{2,1,0:T(2,128)S(1)}, u32[]{:S(2)}, u32[]{:S(2)}) %collective-permute-start.16) | collective-permute-done | bytes 4128 | tf_op jit(solution)/shard_map/ppermute | solution.py:212
  66.0 8.4 %shard_map.106.refs_8_ = f32[16,2,128,1024]{3,2,1,0:T(8,128)} custom-call(s32[1]{0:T(128)} %bitcast.core, bf16[128,3072]{1,0:T(8,128)(2,1)} %collective-permute-done.refs_0_, bf16[128,3072]{1,0:T(8,128)(2,1)} %collective-permute-done.1.refs_1_, bf16[128,3072]{1,0:T(8,128)(2,1)S(1)} %collective-permute-done.14.refs_2_, ...), custom_call_target="tpu_custom_call", output_to_operand_aliasing={{}: (9, {})} | custom-call | flops 3221225472 | bytes 17825792 | tf_op jit(solution)/shard_map/pallas_call | solution.py:54
  79.1 8.5 %shard_map.107.refs_8_ = f32[16,2,128,1024]{3,2,1,0:T(8,128)} custom-call(s32[1]{0:T(128)} %bitcast.core, bf16[128,3072]{1,0:T(8,128)(2,1)S(1)} %collective-permute-done.12.refs_0_, bf16[128,3072]{1,0:T(8,128)(2,1)S(1)} %collective-permute-done.13.refs_1_, bf16[128,3072]{1,0:T(8,128)(2,1)} %collective-permute-done.17.refs_2_, ...), custom_call_target="tpu_custom_call", output_to_operand_aliasing={{}: (9, {})} | custom-call | flops 3221225472 | bytes 17825792 | tf_op jit(solution)/shard_map/pallas_call | solution.py:54
  87.6 7.1 %collective-permute-done.10.refs_0_ = bf16[128,3072]{1,0:T(8,128)(2,1)S(1)} collective-permute-done((bf16[128,3072]{1,0:T(8,128)(2,1)}, bf16[128,3072]{1,0:T(8,128)(2,1)S(1)}, u32[]{:S(2)}, u32[]{:S(2)}) %collective-permute-start.10) | collective-permute-done | bytes 786464 | tf_op jit(solution)/shard_map/ppermute | solution.py:182
  101.9 15.4 %collective-permute-done.25 = f32[4,2,256]{2,1,0:T(2,128)S(1)} collective-permute-done((f32[4,2,256]{2,1,0:T(2,128)S(1)}, f32[4,2,256]{2,1,0:T(2,128)S(1)}, u32[]{:S(2)}, u32[]{:S(2)}) %collective-permute-start.25) | collective-permute-done | bytes 8224 | tf_op jit(solution)/shard_map/ppermute | solution.py:212
  117.3 8.5 %shard_map.108.refs_8_ = f32[16,2,128,1024]{3,2,1,0:T(8,128)} custom-call(s32[1]{0:T(128)} %bitcast.core, bf16[128,3072]{1,0:T(8,128)(2,1)S(1)} %collective-permute-done.10.refs_0_, bf16[128,3072]{1,0:T(8,128)(2,1)S(1)} %collective-permute-done.11.refs_1_, bf16[128,3072]{1,0:T(8,128)(2,1)} %collective-permute-done.23.refs_2_, ...), custom_call_target="tpu_custom_call", output_to_operand_aliasing={{}: (9, {})} | custom-call | flops 3221225472 | bytes 17825792 | tf_op jit(solution)/shard_map/pallas_call | solution.py:54
  130.5 9.0 %shard_map.109.refs_8_ = f32[16,2,128,1024]{3,2,1,0:T(8,128)} custom-call(s32[1]{0:T(128)} %bitcast.core, bf16[128,3072]{1,0:T(8,128)(2,1)} %collective-permute-done.21.refs_0_, bf16[128,3072]{1,0:T(8,128)(2,1)} %collective-permute-done.22.refs_1_, bf16[128,3072]{1,0:T(8,128)(2,1)} %collective-permute-done.26.refs_2_, ...), custom_call_target="tpu_custom_call", output_to_operand_aliasing={{}: (9, {})} | custom-call | flops 3221225472 | bytes 17825792 | tf_op jit(solution)/shard_map/pallas_call | solution.py:54
  139.5 6.4 %collective-permute-done.19.refs_0_ = bf16[128,3072]{1,0:T(8,128)(2,1)S(1)} collective-permute-done((bf16[128,3072]{1,0:T(8,128)(2,1)S(1)}, bf16[128,3072]{1,0:T(8,128)(2,1)S(1)}, u32[]{:S(2)}, u32[]{:S(2)}) %collective-permute-start.19) | collective-permute-done | bytes 786464 | tf_op jit(solution)/shard_map/ppermute | solution.py:182
  152.5 7.7 %shard_map.110.refs_8_ = f32[16,2,128,1024]{3,2,1,0:T(8,128)} custom-call(s32[1]{0:T(128)} %bitcast.core, bf16[128,3072]{1,0:T(8,128)(2,1)S(1)} %collective-permute-done.19.refs_0_, bf16[128,3072]{1,0:T(8,128)(2,1)S(1)} %collective-permute-done.20.refs_1_, bf16[128,3072]{1,0:T(8,128)(2,1)S(1)} %collective-permute-done.32.refs_2_, ...), custom_call_target="tpu_custom_call", output_to_operand_aliasing={{}: (9, {})} | custom-call | flops 3221225472 | bytes 17825792 | tf_op jit(solution)/shard_map/pallas_call | solution.py:54
  160.1 6.2 %collective-permute-done.30.refs_0_ = bf16[128,3072]{1,0:T(8,128)(2,1)S(1)} collective-permute-done((bf16[128,3072]{1,0:T(8,128)(2,1)}, bf16[128,3072]{1,0:T(8,128)(2,1)S(1)}, u32[]{:S(2)}, u32[]{:S(2)}) %collective-permute-start.30) | collective-permute-done | bytes 786464 | tf_op jit(solution)/shard_map/ppermute | solution.py:182
  173.6 7.7 %shard_map.111.refs_8_ = f32[16,2,128,1024]{3,2,1,0:T(8,128)} custom-call(s32[1]{0:T(128)} %bitcast.core, bf16[128,3072]{1,0:T(8,128)(2,1)S(1)} %collective-permute-done.30.refs_0_, bf16[128,3072]{1,0:T(8,128)(2,1)S(1)} %collective-permute-done.31.refs_1_, bf16[128,3072]{1,0:T(8,128)(2,1)S(1)} %collective-permute-done.34.refs_2_, ...), custom_call_target="tpu_custom_call", output_to_operand_aliasing={{}: (9, {})} | custom-call | flops 3221225472 | bytes 17825792 | tf_op jit(solution)/shard_map/pallas_call | solution.py:54
  181.3 6.1 %collective-permute-done.28.refs_0_ = bf16[128,3072]{1,0:T(8,128)(2,1)S(1)} collective-permute-done((bf16[128,3072]{1,0:T(8,128)(2,1)S(1)}, bf16[128,3072]{1,0:T(8,128)(2,1)S(1)}, u32[]{:S(2)}, u32[]{:S(2)}) %collective-permute-start.28) | collective-permute-done | bytes 786464 | tf_op jit(solution)/shard_map/ppermute | solution.py:182
  194.0 7.6 %shard_map.112 = f32[16,2,128,1024]{3,2,1,0:T(8,128)} custom-call(s32[1]{0:T(128)} %bitcast.core, bf16[128,3072]{1,0:T(8,128)(2,1)S(1)} %collective-permute-done.28.refs_0_, bf16[128,3072]{1,0:T(8,128)(2,1)S(1)} %collective-permute-done.29.refs_1_, bf16[128,3072]{1,0:T(8,128)(2,1)S(1)} %collective-permute-done.36.refs_2_, ...), custom_call_target="tpu_custom_call", output_to_operand_aliasing={{}: (9, {})} | custom-call | flops 3221225472 | bytes 17825792 | tf_op jit(solution)/shard_map/pallas_call | solution.py:54
  210.0 4.5 %collective-permute-done.41 = f16[2,128,1024]{2,1,0:T(8,128)(2,1)S(1)} collective-permute-done((f16[2,128,1024]{2,1,0:T(8,128)(2,1)}, f16[2,128,1024]{2,1,0:T(8,128)(2,1)S(1)}, u32[]{:S(2)}, u32[]{:S(2)}) %collective-permute-start.41) | collective-permute-done | bytes 524320 | tf_op jit(solution)/shard_map/ppermute | solution.py:245
  215.9 9.8 %collective-permute-done.42 = f16[2,128,1024]{2,1,0:T(8,128)(2,1)S(1)} collective-permute-done((f16[2,128,1024]{2,1,0:T(8,128)(2,1)}, f16[2,128,1024]{2,1,0:T(8,128)(2,1)S(1)}, u32[]{:S(2)}, u32[]{:S(2)}) %collective-permute-start.42) | collective-permute-done | bytes 524320 | tf_op jit(solution)/shard_map/ppermute | solution.py:245
  227.1 8.8 %collective-permute-done.43 = f16[2,128,1024]{2,1,0:T(8,128)(2,1)S(1)} collective-permute-done((f16[2,128,1024]{2,1,0:T(8,128)(2,1)}, f16[2,128,1024]{2,1,0:T(8,128)(2,1)S(1)}, u32[]{:S(2)}, u32[]{:S(2)}) %collective-permute-start.43) | collective-permute-done | bytes 524320 | tf_op jit(solution)/shard_map/ppermute | solution.py:245
  238.3 3.2 %select_reduce_fusion = (f32[8,128]{1,0:T(8,128)S(1)}, f32[8,128]{1,0:T(8,128)S(1)}, f32[8,128]{1,0:T(8,128)S(1)}, f32[8,128]{1,0:T(8,128)S(1)}) fusion(f32[8,2,128,1024]{3,2,1,0:T(8,128)S(1)} %bitcast_dynamic-update-slice_fusion.2, s32[8,128]{1,0:T(8,128)S(1)} %add_subtract_fusion, f32[8,128]{1,0:T(8,128)S(1)} %bitcast.544, ...), kind=kLoop, calls=%fused_computation.4 | loop fusion | flops 12578816 | bytes 8425472 | tf_op jit(solution)/shard_map/reduce_sum | solution.py:299
  243.7 12.7 %collective-permute-done.44 = f16[2,128,1024]{2,1,0:T(8,128)(2,1)S(1)} collective-permute-done((f16[2,128,1024]{2,1,0:T(8,128)(2,1)S(1)}, f16[2,128,1024]{2,1,0:T(8,128)(2,1)S(1)}, u32[]{:S(2)}, u32[]{:S(2)}) %collective-permute-start.44) | collective-permute-done | bytes 524320 | tf_op jit(solution)/shard_map/ppermute | solution.py:245
  258.1 3.1 %copy-done.2 = f32[8,2,128,1024]{3,2,1,0:T(8,128)} copy-done((f32[8,2,128,1024]{3,2,1,0:T(8,128)}, f32[8,2,128,1024]{3,2,1,0:T(8,128)S(1)}, u32[]{:S(2)}) %copy-start.2) | copy-done | bytes 8388632
  261.7 4.1 %collective-permute-done.45 = f16[2,128,1024]{2,1,0:T(8,128)(2,1)S(1)} collective-permute-done((f16[2,128,1024]{2,1,0:T(8,128)(2,1)}, f16[2,128,1024]{2,1,0:T(8,128)(2,1)S(1)}, u32[]{:S(2)}, u32[]{:S(2)}) %collective-permute-start.45) | collective-permute-done | bytes 524320 | tf_op jit(solution)/shard_map/ppermute | solution.py:245
  277.7 5.0 %slice_bitcast_fusion.3 = (f32[4,128,1024]{2,1,0:T(8,128)}, f32[4,1,128,1024]{3,2,1,0:T(8,128)S(1)}, f32[4,1,128,1024]{3,2,1,0:T(8,128)S(1)}) fusion(f32[8,2,128,1024]{3,2,1,0:T(8,128)} %bitcast_dynamic-update-slice_fusion), kind=kLoop, calls=%fused_computation.25 | loop fusion | bytes 12582912 | tf_op jit(solution)/shard_map/squeeze | solution.py:329
  (215 shorter events, 105.0 us)
Async XLA Ops:
  3.5 22.9 %collective-permute-start.8 = (bf16[2048,1024]{1,0:T(8,128)(2,1)S(1)}, bf16[2048,1024]{1,0:T(8,128)(2,1)S(1)}, u32[]{:S(2)}, u32[]{:S(2)}) collective-permute-start(bf16[2048,1024]{1,0:T(8,128)(2,1)S(1)} %constant_dynamic-slice_fusion.9), channel_id=1, source_target_pairs={{0,16},{16,0},{1,17},{17,1},{2,18},{18,2},{3,19},{19,3},{4,20},{20... | collective-permute-start | bytes 12582920 | tf_op jit(solution)/shard_map/ppermute | solution.py:164
  4.4 22.0 %collective-permute-start.9 = (bf16[1024,1024]{1,0:T(8,128)(2,1)S(1)}, bf16[1024,1024]{1,0:T(8,128)(2,1)S(1)}, u32[]{:S(2)}, u32[]{:S(2)}) collective-permute-start(bf16[1024,1024]{1,0:T(8,128)(2,1)S(1)} %constant_dynamic-slice_fusion.8), channel_id=1, source_target_pairs={{0,16},{16,0},{1,17},{17,1},{2,18},{18,2},{3,19},{19,3},{4,20},{20... | collective-permute-start | bytes 6291464 | tf_op jit(solution)/shard_map/ppermute | solution.py:164
  5.4 20.9 %collective-permute-start.6 = (bf16[128,3072]{1,0:T(8,128)(2,1)S(1)}, bf16[128,3072]{1,0:T(8,128)(2,1)S(1)}, u32[]{:S(2)}, u32[]{:S(2)}) collective-permute-start(bf16[128,3072]{1,0:T(8,128)(2,1)S(1)} %get-tuple-element.60.refs_0_), channel_id=1, source_target_pairs={{0,16},{16,0},{1,17},{17,1},{2,18},{18,2},{3,19},{19,3},{4,20},{20... | collective-permute-start | bytes 2359304 | tf_op jit(solution)/shard_map/ppermute | solution.py:164
  6.5 19.8 %collective-permute-start.7 = (bf16[128,3072]{1,0:T(8,128)(2,1)S(1)}, bf16[128,3072]{1,0:T(8,128)(2,1)S(1)}, u32[]{:S(2)}, u32[]{:S(2)}) collective-permute-start(bf16[128,3072]{1,0:T(8,128)(2,1)S(1)} %get-tuple-element.61.refs_1_), channel_id=1, source_target_pairs={{0,16},{16,0},{1,17},{17,1},{2,18},{18,2},{3,19},{19,3},{4,20},{20... | collective-permute-start | bytes 2359304 | tf_op jit(solution)/shard_map/ppermute | solution.py:164
  44.6 21.3 %collective-permute-start.14 = (bf16[128,3072]{1,0:T(8,128)(2,1)}, bf16[128,3072]{1,0:T(8,128)(2,1)S(1)}, u32[]{:S(2)}, u32[]{:S(2)}) collective-permute-start(bf16[128,3072]{1,0:T(8,128)(2,1)} %collective-permute-done.refs_0_), channel_id=1, source_target_pairs={{0,16},{16,0},{1,17},{17,1},{2,18},{18,2},{3,19},{19,3},{4,20},{20... | collective-permute-start | bytes 2359304 | tf_op jit(solution)/shard_map/ppermute | solution.py:164
  44.6 21.3 %collective-permute-start.15 = (bf16[128,3072]{1,0:T(8,128)(2,1)}, bf16[128,3072]{1,0:T(8,128)(2,1)S(1)}, u32[]{:S(2)}, u32[]{:S(2)}) collective-permute-start(bf16[128,3072]{1,0:T(8,128)(2,1)} %collective-permute-done.1.refs_1_), channel_id=1, source_target_pairs={{0,16},{16,0},{1,17},{17,1},{2,18},{18,2},{3,19},{19,3},{4,20},{20... | collective-permute-start | bytes 2359304 | tf_op jit(solution)/shard_map/ppermute | solution.py:164
  45.1 29.3 %collective-permute-start.12 = (bf16[128,3072]{1,0:T(8,128)(2,1)S(1)}, bf16[128,3072]{1,0:T(8,128)(2,1)S(1)}, u32[]{:S(2)}, u32[]{:S(2)}) collective-permute-start(bf16[128,3072]{1,0:T(8,128)(2,1)S(1)} %get-tuple-element.61.refs_1_), channel_id=1, source_target_pairs={{0,4},{4,8},{8,12},{12,14},{14,10},{10,6},{6,2},{2,0},{1,5},{5,9},... | collective-permute-start | bytes 2359304 | tf_op jit(solution)/shard_map/ppermute | solution.py:182
  46.7 27.7 %collective-permute-start.13 = (bf16[128,3072]{1,0:T(8,128)(2,1)S(1)}, bf16[128,3072]{1,0:T(8,128)(2,1)S(1)}, u32[]{:S(2)}, u32[]{:S(2)}) collective-permute-start(bf16[128,3072]{1,0:T(8,128)(2,1)S(1)} %get-tuple-element.60.refs_0_), channel_id=1, source_target_pairs={{4,0},{8,4},{12,8},{14,12},{10,14},{6,10},{2,6},{0,2},{5,1},{9,5},... | collective-permute-start | bytes 2359304 | tf_op jit(solution)/shard_map/ppermute | solution.py:183
  75.0 19.7 %collective-permute-start.10 = (bf16[128,3072]{1,0:T(8,128)(2,1)}, bf16[128,3072]{1,0:T(8,128)(2,1)S(1)}, u32[]{:S(2)}, u32[]{:S(2)}) collective-permute-start(bf16[128,3072]{1,0:T(8,128)(2,1)} %collective-permute-done.refs_0_), channel_id=1, source_target_pairs={{0,4},{4,8},{8,12},{12,14},{14,10},{10,6},{6,2},{2,0},{1,5},{5,9},... | collective-permute-start | bytes 2359304 | tf_op jit(solution)/shard_map/ppermute | solution.py:182
  75.3 20.5 %collective-permute-start.11 = (bf16[128,3072]{1,0:T(8,128)(2,1)}, bf16[128,3072]{1,0:T(8,128)(2,1)S(1)}, u32[]{:S(2)}, u32[]{:S(2)}) collective-permute-start(bf16[128,3072]{1,0:T(8,128)(2,1)} %collective-permute-done.1.refs_1_), channel_id=1, source_target_pairs={{4,0},{8,4},{12,8},{14,12},{10,14},{6,10},{2,6},{0,2},{5,1},{9,5},... | collective-permute-start | bytes 2359304 | tf_op jit(solution)/shard_map/ppermute | solution.py:183
  95.8 21.5 %collective-permute-start.23 = (bf16[128,3072]{1,0:T(8,128)(2,1)S(1)}, bf16[128,3072]{1,0:T(8,128)(2,1)}, u32[]{:S(2)}, u32[]{:S(2)}) collective-permute-start(bf16[128,3072]{1,0:T(8,128)(2,1)S(1)} %collective-permute-done.10.refs_0_), channel_id=1, source_target_pairs={{0,16},{16,0},{1,17},{17,1},{2,18},{18,2},{3,19},{19,3},{4,20},{20... | collective-permute-start | bytes 2359304 | tf_op jit(solution)/shard_map/ppermute | solution.py:164
  95.8 21.5 %collective-permute-start.24 = (bf16[128,3072]{1,0:T(8,128)(2,1)S(1)}, bf16[128,3072]{1,0:T(8,128)(2,1)}, u32[]{:S(2)}, u32[]{:S(2)}) collective-permute-start(bf16[128,3072]{1,0:T(8,128)(2,1)S(1)} %collective-permute-done.11.refs_1_), channel_id=1, source_target_pairs={{0,16},{16,0},{1,17},{17,1},{2,18},{18,2},{3,19},{19,3},{4,20},{20... | collective-permute-start | bytes 2359304 | tf_op jit(solution)/shard_map/ppermute | solution.py:164
  96.3 29.5 %collective-permute-start.21 = (bf16[128,3072]{1,0:T(8,128)(2,1)S(1)}, bf16[128,3072]{1,0:T(8,128)(2,1)}, u32[]{:S(2)}, u32[]{:S(2)}) collective-permute-start(bf16[128,3072]{1,0:T(8,128)(2,1)S(1)} %collective-permute-done.12.refs_0_), channel_id=1, source_target_pairs={{0,4},{4,8},{8,12},{12,14},{14,10},{10,6},{6,2},{2,0},{1,5},{5,9},... | collective-permute-start | bytes 2359304 | tf_op jit(solution)/shard_map/ppermute | solution.py:182
  98.0 27.7 %collective-permute-start.22 = (bf16[128,3072]{1,0:T(8,128)(2,1)S(1)}, bf16[128,3072]{1,0:T(8,128)(2,1)}, u32[]{:S(2)}, u32[]{:S(2)}) collective-permute-start(bf16[128,3072]{1,0:T(8,128)(2,1)S(1)} %collective-permute-done.13.refs_1_), channel_id=1, source_target_pairs={{4,0},{8,4},{12,8},{14,12},{10,14},{6,10},{2,6},{0,2},{5,1},{9,5},... | collective-permute-start | bytes 2359304 | tf_op jit(solution)/shard_map/ppermute | solution.py:183
  126.3 19.5 %collective-permute-start.19 = (bf16[128,3072]{1,0:T(8,128)(2,1)S(1)}, bf16[128,3072]{1,0:T(8,128)(2,1)S(1)}, u32[]{:S(2)}, u32[]{:S(2)}) collective-permute-start(bf16[128,3072]{1,0:T(8,128)(2,1)S(1)} %collective-permute-done.10.refs_0_), channel_id=1, source_target_pairs={{0,4},{4,8},{8,12},{12,14},{14,10},{10,6},{6,2},{2,0},{1,5},{5,9},... | collective-permute-start | bytes 2359304 | tf_op jit(solution)/shard_map/ppermute | solution.py:182
  146.6 19.7 %collective-permute-start.30 = (bf16[128,3072]{1,0:T(8,128)(2,1)}, bf16[128,3072]{1,0:T(8,128)(2,1)S(1)}, u32[]{:S(2)}, u32[]{:S(2)}) collective-permute-start(bf16[128,3072]{1,0:T(8,128)(2,1)} %collective-permute-done.21.refs_0_), channel_id=1, source_target_pairs={{0,4},{4,8},{8,12},{12,14},{14,10},{10,6},{6,2},{2,0},{1,5},{5,9},... | collective-permute-start | bytes 2359304 | tf_op jit(solution)/shard_map/ppermute | solution.py:182
  148.7 56.4 %collective-permute-start.38 = (f16[2,128,1024]{2,1,0:T(8,128)(2,1)}, f16[2,128,1024]{2,1,0:T(8,128)(2,1)S(1)}, u32[]{:S(2)}, u32[]{:S(2)}) collective-permute-start(f16[2,128,1024]{2,1,0:T(8,128)(2,1)} %fusion.14), channel_id=1, source_target_pairs={{0,1},{1,0},{2,3},{3,2},{4,5},{5,4},{6,7},{7,6},{8,9},{9,8},{10,11... | collective-permute-start | bytes 1572872 | tf_op jit(solution)/shard_map/ppermute | solution.py:245
  167.9 19.5 %collective-permute-start.28 = (bf16[128,3072]{1,0:T(8,128)(2,1)S(1)}, bf16[128,3072]{1,0:T(8,128)(2,1)S(1)}, u32[]{:S(2)}, u32[]{:S(2)}) collective-permute-start(bf16[128,3072]{1,0:T(8,128)(2,1)S(1)} %collective-permute-done.19.refs_0_), channel_id=1, source_target_pairs={{0,4},{4,8},{8,12},{12,14},{14,10},{10,6},{6,2},{2,0},{1,5},{5,9},... | collective-permute-start | bytes 2359304 | tf_op jit(solution)/shard_map/ppermute | solution.py:182
  172.1 34.9 %collective-permute-start.39 = (f16[2,128,1024]{2,1,0:T(8,128)(2,1)}, f16[2,128,1024]{2,1,0:T(8,128)(2,1)S(1)}, u32[]{:S(2)}, u32[]{:S(2)}) collective-permute-start(f16[2,128,1024]{2,1,0:T(8,128)(2,1)} %fusion.15), channel_id=1, source_target_pairs={{0,1},{1,0},{2,3},{3,2},{4,5},{5,4},{6,7},{7,6},{8,9},{9,8},{10,11... | collective-permute-start | bytes 1572872 | tf_op jit(solution)/shard_map/ppermute | solution.py:245
  188.2 20.4 %collective-permute-start.40 = (f16[2,128,1024]{2,1,0:T(8,128)(2,1)}, f16[2,128,1024]{2,1,0:T(8,128)(2,1)S(1)}, u32[]{:S(2)}, u32[]{:S(2)}) collective-permute-start(f16[2,128,1024]{2,1,0:T(8,128)(2,1)} %fusion.16), channel_id=1, source_target_pairs={{0,1},{1,0},{2,3},{3,2},{4,5},{5,4},{6,7},{7,6},{8,9},{9,8},{10,11... | collective-permute-start | bytes 1572872 | tf_op jit(solution)/shard_map/ppermute | solution.py:245
  192.0 22.5 %collective-permute-start.41 = (f16[2,128,1024]{2,1,0:T(8,128)(2,1)}, f16[2,128,1024]{2,1,0:T(8,128)(2,1)S(1)}, u32[]{:S(2)}, u32[]{:S(2)}) collective-permute-start(f16[2,128,1024]{2,1,0:T(8,128)(2,1)} %fusion.17), channel_id=1, source_target_pairs={{0,1},{1,0},{2,3},{3,2},{4,5},{5,4},{6,7},{7,6},{8,9},{9,8},{10,11... | collective-permute-start | bytes 1572872 | tf_op jit(solution)/shard_map/ppermute | solution.py:245
  192.5 33.2 %collective-permute-start.42 = (f16[2,128,1024]{2,1,0:T(8,128)(2,1)}, f16[2,128,1024]{2,1,0:T(8,128)(2,1)S(1)}, u32[]{:S(2)}, u32[]{:S(2)}) collective-permute-start(f16[2,128,1024]{2,1,0:T(8,128)(2,1)} %fusion.18), channel_id=1, source_target_pairs={{0,1},{1,0},{2,3},{3,2},{4,5},{5,4},{6,7},{7,6},{8,9},{9,8},{10,11... | collective-permute-start | bytes 1572872 | tf_op jit(solution)/shard_map/ppermute | solution.py:245
  205.1 30.9 %collective-permute-start.43 = (f16[2,128,1024]{2,1,0:T(8,128)(2,1)}, f16[2,128,1024]{2,1,0:T(8,128)(2,1)S(1)}, u32[]{:S(2)}, u32[]{:S(2)}) collective-permute-start(f16[2,128,1024]{2,1,0:T(8,128)(2,1)} %fusion.19), channel_id=1, source_target_pairs={{0,1},{1,0},{2,3},{3,2},{4,5},{5,4},{6,7},{7,6},{8,9},{9,8},{10,11... | collective-permute-start | bytes 1572872 | tf_op jit(solution)/shard_map/ppermute | solution.py:245
  243.2 22.7 %collective-permute-start.45 = (f16[2,128,1024]{2,1,0:T(8,128)(2,1)}, f16[2,128,1024]{2,1,0:T(8,128)(2,1)S(1)}, u32[]{:S(2)}, u32[]{:S(2)}) collective-permute-start(f16[2,128,1024]{2,1,0:T(8,128)(2,1)} %fusion.21), channel_id=1, source_target_pairs={{0,1},{1,0},{2,3},{3,2},{4,5},{5,4},{6,7},{7,6},{8,9},{9,8},{10,11... | collective-permute-start | bytes 1572872 | tf_op jit(solution)/shard_map/ppermute | solution.py:245
  (41 other events, 321.4 us)
